TPU v7x, 32 devices: a whole 2x2x4 slice. The times are simulated.
32 devices in a mesh: tile: 8 (over y, x, core), depth: 4 (over z).
Axes of the slice: x: 2, y: 2, z: 4, core: 2. Of those that a mesh axis runs over, the one named last changes fastest.
Arguments:
- initial_state: float32 [2, 32, 8192], P(None, 'depth', 'tile'), may hold values from -6 to 6
- observed: float32 [2, 32, 8192], P(None, 'depth', 'tile'), may hold values from -6 to 6
- edge_weight: float32 [8192], P('tile'), may hold values from 0.25 to 1
- land: int32 [8192], P('tile'), may hold values 0 or 1
- w_in: bfloat16 [64, 640], replicated, may hold values from -0.75 to 0.75
- b_in: float32 [640], replicated, may hold values from -3 to 3
- w_mid: bfloat16 [640, 640], replicated, may hold values from -0.25 to 0.25
- b_mid: float32 [640], replicated, may hold values from -3 to 3
- w_out: bfloat16 [640, 64], replicated, may hold values from -0.25 to 0.25
- b_out: float32 [64], replicated, may hold values from -3 to 3
Outputs:
- final_state: float32 [2, 32, 8192], P(None, 'depth', 'tile')
- sensitivity: float32 [2, 32, 8192], P(None, 'depth', 'tile')
- grad_w_in: float32 [64, 640], replicated
- grad_b_in: float32 [640], replicated
- grad_w_mid: float32 [640, 640], replicated
- grad_b_mid: float32 [640], replicated
- grad_w_out: float32 [640, 64], replicated
- grad_b_out: float32 [64], replicated
All inputs are finite; a program needn't handle non-finite values. No bound on the sum of `land` on one device may be relied on, other than what follows from the above.
Results may differ from a plain program's by a relative error of at most 0.0017.
Values may be sent and summed in bfloat16 or wider, within the bound.
No kernel may reach another device: no remote copies, remote signals or barrier semaphores. Data moves between devices by JAX's collectives and lax.ppermute only.
A program may use at most 64 MiB of HBM per device.

v0:
```python
import jax
import jax.numpy as jnp
from jax import lax
from jax.sharding import PartitionSpec as P

TILE_SIDE = 32
LEVELS = 32
TIME_STEPS = 2
FEATURES = 64
TILE_CELLS = 1024
diffuse_coef = 0.2
step_size = 0.5


def with_halo(cells, sides, width):
    for axis, dim in sides:
        count = lax.axis_size(axis)
        head = lax.slice_in_dim(cells, 0, width, axis=dim)
        tail = lax.slice_in_dim(cells, cells.shape[dim] - width, cells.shape[dim], axis=dim)
        cells = jnp.concatenate(
            [
                lax.ppermute(tail, axis, [(i, (i + 1) % count) for i in range(count)]),
                cells,
                lax.ppermute(head, axis, [((i + 1) % count, i) for i in range(count)]),
            ],
            axis=dim,
        )
    return cells


def passed_along(x, axis, by):
    length = lax.axis_size(axis)
    return lax.ppermute(x, axis, [(i, (i + by) % length) for i in range(length)])


def neighbour_sum(flat_rows):
    row_count = flat_rows.shape[0]
    tile_grid = flat_rows.reshape(row_count, TILE_SIDE, TILE_SIDE)
    zonal_pair = jnp.stack([tile_grid[:, :, -1], tile_grid[:, :, 0]], axis=1)
    padded = with_halo(zonal_pair[None], (("tile", 0),), 1)
    from_west = padded[0, :, 0, :]
    from_east = padded[2, :, 1, :]
    fold_pair = jnp.stack([tile_grid[:, 0, :], tile_grid[:, -1, :]], axis=1)
    across = passed_along(fold_pair, "tile", lax.axis_size("tile") // 2)[:, :, ::-1]
    west_cells = jnp.concatenate([from_west[:, :, None], tile_grid[:, :, :-1]], axis=2)
    east_cells = jnp.concatenate([tile_grid[:, :, 1:], from_east[:, :, None]], axis=2)
    south_cells = jnp.concatenate([across[:, 0, None, :], tile_grid[:, :-1, :]], axis=1)
    north_cells = jnp.concatenate([tile_grid[:, 1:, :], across[:, 1, None, :]], axis=1)
    return (west_cells + east_cells + south_cells + north_cells).reshape(row_count, TILE_CELLS)


def diffuse(tracer_field, weight, weight_sums):
    flat_rows = tracer_field.reshape(-1, TILE_CELLS)
    scaled = flat_rows * weight[None, :]
    result_rows = weight[None, :] * (neighbour_sum(scaled) - flat_rows * weight_sums[None, :])
    return result_rows.reshape(tracer_field.shape)


def silu_slope(pre_act):
    sigmoid_val = jax.nn.sigmoid(pre_act)
    return sigmoid_val * (1.0 + pre_act * (1.0 - sigmoid_val))


def closure_forward(inputs, params):
    w_in, b_in, w_mid, b_mid, w_out, b_out = params
    contract_rows = (((0,), (0,)), ((), ()))
    pre_one = (
        lax.dot_general(w_in, inputs, contract_rows, preferred_element_type=jnp.float32)
        + b_in[:, None]
    )
    hidden_one = jax.nn.silu(pre_one).astype(jnp.bfloat16)
    pre_two = (
        lax.dot_general(w_mid, hidden_one, contract_rows, preferred_element_type=jnp.float32)
        + b_mid[:, None]
    )
    hidden_two = jax.nn.silu(pre_two).astype(jnp.bfloat16)
    output = (
        lax.dot_general(w_out, hidden_two, contract_rows, preferred_element_type=jnp.float32)
        + b_out[:, None]
    )
    return (output, (inputs, pre_one, hidden_one, pre_two, hidden_two))


def closure_backward(upstream, saved_cache, params):
    w_in, b_in, w_mid, b_mid, w_out, b_out = params
    inputs, pre_one, hidden_one, pre_two, hidden_two = saved_cache
    contract_cols = (((1,), (1,)), ((), ()))
    grad_w_out = lax.dot_general(
        hidden_two, upstream, contract_cols, preferred_element_type=jnp.float32
    )
    grad_b_out = jnp.sum(upstream.astype(jnp.float32), axis=1)
    slope_two = (
        jnp.dot(w_out, upstream, preferred_element_type=jnp.float32) * silu_slope(pre_two)
    ).astype(jnp.bfloat16)
    grad_w_mid = lax.dot_general(
        hidden_one, slope_two, contract_cols, preferred_element_type=jnp.float32
    )
    grad_b_mid = jnp.sum(slope_two.astype(jnp.float32), axis=1)
    slope_one = (
        jnp.dot(w_mid, slope_two, preferred_element_type=jnp.float32) * silu_slope(pre_one)
    ).astype(jnp.bfloat16)
    grad_w_in = lax.dot_general(
        inputs, slope_one, contract_cols, preferred_element_type=jnp.float32
    )
    grad_b_in = jnp.sum(slope_one.astype(jnp.float32), axis=1)
    back_grad = jnp.dot(w_in, slope_one, preferred_element_type=jnp.float32)
    return (back_grad, (grad_w_in, grad_b_in, grad_w_mid, grad_b_mid, grad_w_out, grad_b_out))


def is_power_of_two(count):
    return count & count - 1 == 0


def swapped(x, axis, even_bit, odd_bit):
    length = lax.axis_size(axis)
    return lax.ppermute(x, axis, [(i, i ^ (odd_bit if i & 1 else even_bit)) for i in range(length)])


def tile_rounds(length):
    bits = [1 << k for k in range(length.bit_length() - 1)]
    rounds = [(bits[0], bits[0])] if bits else []
    rest = bits[1:]
    for k in range(len(rest)):
        rounds.append((rest[k], rest[(k + 1) % len(rest)]))
    return rounds


def all_summed(block):
    tiles = lax.axis_size("tile")
    depths = lax.axis_size("depth")
    if not (is_power_of_two(tiles) and is_power_of_two(depths)):
        return lax.psum(block, ("tile", "depth"))
    width = block.shape[-1]
    tile = lax.axis_index("tile")
    rounds = tile_rounds(tiles)
    sides = []
    for even_bit, odd_bit in rounds:
        bit = jnp.where(tile & 1 == 1, odd_bit, even_bit)
        sides.append((tile & bit != 0).astype(jnp.int32))
    for (even_bit, odd_bit), side in zip(rounds, sides):
        halves = block.reshape(2, -1, width)
        sent = lax.dynamic_index_in_dim(halves, 1 - side, 0, False)
        kept = lax.dynamic_index_in_dim(halves, side, 0, False)
        block = kept + swapped(sent, "tile", even_bit, odd_bit)
    bit = 1
    while bit < depths:
        block = block + swapped(block, "depth", bit, bit)
        bit *= 2
    for (even_bit, odd_bit), side in zip(reversed(rounds), reversed(sides)):
        other = swapped(block, "tile", even_bit, odd_bit)
        block = jnp.where(side == 0, jnp.stack([block, other]), jnp.stack([other, block])).reshape(
            -1, width
        )
    return block


def reduced_gradients(totals):
    grad_w_in, grad_b_in, grad_w_mid, grad_b_mid, grad_w_out, grad_b_out = totals
    width = grad_w_mid.shape[1]
    features = grad_w_in.shape[0]
    bias_rows = jnp.zeros((8, width), jnp.float32)
    bias_rows = (
        bias_rows.at[0].set(grad_b_in).at[1].set(grad_b_mid).at[2, :features].set(grad_b_out)
    )
    parts = [grad_w_mid, grad_w_in, grad_w_out.T, bias_rows]
    rows = sum((part.shape[0] for part in parts))
    step = 8 * lax.axis_size("tile")
    pad = -rows % step
    block = jnp.concatenate(parts + [jnp.zeros((pad, width), jnp.float32)], axis=0)
    block = all_summed(block)
    top = width
    out_in = block[top : top + features]
    out_out = block[top + features : top + 2 * features].T
    biases = block[top + 2 * features : top + 2 * features + 8]
    return (out_in, biases[0], block[:width], biases[1], out_out, biases[2, :features])


def body(initial_state, observed, edge_weight, land, w_in, b_in, w_mid, b_mid, w_out, b_out):
    params = (w_in, b_in, w_mid, b_mid, w_out, b_out)
    ocean_mask = land.astype(jnp.float32)
    weight = edge_weight * ocean_mask
    weight_sums = neighbour_sum(weight[None, :])[0]

    def to_columns(segment):
        full_cols = lax.all_to_all(segment, "depth", split_axis=2, concat_axis=1, tiled=True)
        return full_cols.reshape(FEATURES, full_cols.shape[2])

    def to_segments(values):
        shaped = values.reshape(2, LEVELS, values.shape[1])
        segment_part = lax.all_to_all(shaped, "depth", split_axis=1, concat_axis=2, tiled=True)
        return segment_part

    state_now = initial_state
    caches = []
    for step_index in range(TIME_STEPS):
        inputs = to_columns(state_now.astype(jnp.bfloat16))
        tendency, saved_cache = closure_forward(inputs, params)
        caches.append(saved_cache)
        change = diffuse(state_now, weight, weight_sums)
        state_now = (
            state_now
            + diffuse_coef * change
            + step_size * ocean_mask[None, None, :] * to_segments(tendency)
        )
    adjoint = ocean_mask[None, None, :] * (state_now - observed)
    grad_list = []
    for step_index in reversed(range(TIME_STEPS)):
        upstream = to_columns(
            (step_size * ocean_mask[None, None, :] * adjoint).astype(jnp.bfloat16)
        )
        back_grad, param_grads = closure_backward(upstream, caches[step_index], params)
        grad_list.append(param_grads)
        spread = diffuse(adjoint, weight, weight_sums)
        adjoint = adjoint + diffuse_coef * spread + to_segments(back_grad)
    totals = grad_list[0]
    for param_grads in grad_list[1:]:
        totals = tuple((total + gradient for total, gradient in zip(totals, param_grads)))
    summed = reduced_gradients(totals)
    grad_scale = 1.0 / (lax.axis_size("tile") * TILE_CELLS)
    return (
        state_now,
        adjoint,
        summed[0] * grad_scale,
        summed[1] * grad_scale,
        summed[2] * grad_scale,
        summed[3] * grad_scale,
        summed[4] * grad_scale,
        summed[5] * grad_scale,
    )


def solution(mesh):
    return jax.shard_map(
        body,
        mesh=mesh,
        in_specs=(
            P(None, "depth", "tile"),
            P(None, "depth", "tile"),
            P("tile"),
            P("tile"),
            P(),
            P(),
            P(),
            P(),
            P(),
            P(),
        ),
        out_specs=(
            P(None, "depth", "tile"),
            P(None, "depth", "tile"),
            P(),
            P(),
            P(),
            P(),
            P(),
            P(),
        ),
        check_vma=False,
    )
```

profile of v0, /device:TPU:0, one launch (start us, length us, event | category | flops | bytes accessed | tf_op | source)
XLA Modules:
  0.0 191.3 jit_solution(9956939731741169588)
XLA Ops:
  1.7 3.4 %collective-permute-start.4 = (f32[1,1,2,32]{3,2,1,0:T(2,128)S(1)}, f32[1,1,2,32]{3,2,1,0:T(2,128)S(1)}, u32[]{:S(2)}, u32[]{:S(2)}) collective-permute-start(f32[1,1,2,32]{3,2,1,0:T(2,128)S(1)} %maximum_bitcast_fusion.4), channel_id=1, source_target_pairs={{4,0},{8,4},{12,8},{16,12},{20,16},{24,20},{28,24},{0,28},{5,1},{9... | collective-permute-start | bytes 776 | tf_op jit(solution)/shard_map/ppermute | solution.py:24
  6.5 2.7 %collective-permute-start.1 = (f32[1,16,2,32]{3,1,2,0:T(8,128)S(1)}, f32[1,16,2,32]{3,1,2,0:T(8,128)S(1)}, u32[]{:S(2)}, u32[]{:S(2)}) collective-permute-start(f32[1,16,2,32]{3,1,2,0:T(8,128)S(1)} %maximum_bitcast_fusion), channel_id=1, source_target_pairs={{4,0},{8,4},{12,8},{16,12},{20,16},{24,20},{28,24},{0,28},{5,1},{9... | collective-permute-start | bytes 12296 | tf_op jit(solution)/shard_map/ppermute | solution.py:24
  12.1 4.9 %all-to-all-start = ((bf16[4,2,2048]{2,1,0:T(2,128)(2,1)}), bf16[4,2,2048]{2,1,0:T(2,128)(2,1)S(1)}, u32[]{:S(2)}, u32[]{:S(2)}) async-start(bf16[4,2,2048]{2,1,0:T(2,128)(2,1)} %reshape.430), calls=%async_computation | async-start | bytes 65536 | tf_op jit(solution)/shard_map/all_to_all | solution.py:185
  17.9 1.6 collective-permute-start.2
  20.1 1.7 collective-permute-done.2
  24.3 2.1 %multiply_convert_fusion.2 = (bf16[640,256]{0,1:T(8,128)(2,1)S(1)}, f32[640,256]{0,1:T(8,128)}) fusion(f32[640]{0:T(1024)} %param.23, bf16[640,640]{1,0:T(8,128)(2,1)S(1)} %copy-done, f32[640,256]{0,1:T(8,128)S(1)} %convolution_add_fusion.3), kind=kOutput, calls=%fused_computation.40 | convolution fusion | flops 211517440 | bytes 2460160 | tf_op jit(solution)/shard_map/dot_general | solution.py:73
  27.3 4.8 %all-to-all-start.1 = ((f32[2,32,256]{2,0,1:T(2,128)}), f32[2,32,256]{2,0,1:T(2,128)S(1)}, u32[]{:S(2)}, u32[]{:S(2)}) async-start(f32[2,32,256]{2,0,1:T(2,128)} %copy.161), calls=%async_computation.1 | async-start | bytes 131072 | tf_op jit(solution)/shard_map/all_to_all | solution.py:190
  32.5 5.4 %all-to-all-done.1 = f32[2,32,256]{2,0,1:T(2,128)S(1)} async-done(((f32[2,32,256]{2,0,1:T(2,128)}), f32[2,32,256]{2,0,1:T(2,128)S(1)}, u32[]{:S(2)}, u32[]{:S(2)}) %all-to-all-start.1) | async-done | bytes 65568 | tf_op jit(solution)/shard_map/all_to_all | solution.py:190
  39.2 1.6 collective-permute-start.8
  43.0 3.3 %all-to-all-start.2 = ((bf16[4,2,2048]{2,1,0:T(2,128)(2,1)}), bf16[4,2,2048]{2,1,0:T(2,128)(2,1)S(1)}, u32[]{:S(2)}, u32[]{:S(2)}) async-start(bf16[4,2,2048]{2,1,0:T(2,128)(2,1)} %reshape.432), calls=%async_computation.2 | async-start | bytes 65536 | tf_op jit(solution)/shard_map/all_to_all | solution.py:185
  48.1 3.8 %all-to-all-done.2 = bf16[4,2,2048]{2,1,0:T(2,128)(2,1)S(1)} async-done(((bf16[4,2,2048]{2,1,0:T(2,128)(2,1)}), bf16[4,2,2048]{2,1,0:T(2,128)(2,1)S(1)}, u32[]{:S(2)}, u32[]{:S(2)}) %all-to-all-start.2) | async-done | bytes 32800 | tf_op jit(solution)/shard_map/all_to_all | solution.py:185
  53.2 2.3 %multiply_convert_fusion = (bf16[640,256]{0,1:T(8,128)(2,1)S(1)}, f32[640,256]{0,1:T(8,128)}) fusion(f32[640]{0:T(1024)} %param.23, bf16[640,640]{1,0:T(8,128)(2,1)S(1)} %copy-done, f32[640,256]{0,1:T(8,128)S(1)} %fusion.3), kind=kOutput, calls=%fused_computation.36 | convolution fusion | flops 211517440 | bytes 2460160 | tf_op jit(solution)/shard_map/dot_general | solution.py:73
  56.4 3.9 %all-to-all-start.3 = ((f32[2,32,256]{2,0,1:T(2,128)}), f32[2,32,256]{2,0,1:T(2,128)}, u32[]{:S(2)}, u32[]{:S(2)}) async-start(f32[2,32,256]{2,0,1:T(2,128)} %copy.168), calls=%async_computation.3 | async-start | bytes 131072 | tf_op jit(solution)/shard_map/all_to_all | solution.py:190
  61.4 4.7 %all-to-all-done.3 = f32[2,32,256]{2,0,1:T(2,128)} async-done(((f32[2,32,256]{2,0,1:T(2,128)}), f32[2,32,256]{2,0,1:T(2,128)}, u32[]{:S(2)}, u32[]{:S(2)}) %all-to-all-start.3) | async-done | bytes 65568 | tf_op jit(solution)/shard_map/all_to_all | solution.py:190
  71.9 3.4 %all-to-all-start.4 = ((bf16[4,2,2048]{2,1,0:T(2,128)(2,1)}), bf16[4,2,2048]{2,1,0:T(2,128)(2,1)S(1)}, u32[]{:S(2)}, u32[]{:S(2)}) async-start(bf16[4,2,2048]{2,1,0:T(2,128)(2,1)} %reshape.434), calls=%async_computation.4 | async-start | bytes 65536 | tf_op jit(solution)/shard_map/all_to_all | solution.py:185
  76.3 4.6 %all-to-all-done.4 = bf16[4,2,2048]{2,1,0:T(2,128)(2,1)S(1)} async-done(((bf16[4,2,2048]{2,1,0:T(2,128)(2,1)}), bf16[4,2,2048]{2,1,0:T(2,128)(2,1)S(1)}, u32[]{:S(2)}, u32[]{:S(2)}) %all-to-all-start.4) | async-done | bytes 32800 | tf_op jit(solution)/shard_map/all_to_all | solution.py:185
  83.9 1.7 fusion.28
  86.5 3.3 %all-to-all-start.5 = ((f32[2,32,256]{2,0,1:T(2,128)}), f32[2,32,256]{2,0,1:T(2,128)S(1)}, u32[]{:S(2)}, u32[]{:S(2)}) async-start(f32[2,32,256]{2,0,1:T(2,128)} %copy.175), calls=%async_computation.5 | async-start | bytes 131072 | tf_op jit(solution)/shard_map/all_to_all | solution.py:190
  90.0 5.5 %all-to-all-done.5 = f32[2,32,256]{2,0,1:T(2,128)S(1)} async-done(((f32[2,32,256]{2,0,1:T(2,128)}), f32[2,32,256]{2,0,1:T(2,128)S(1)}, u32[]{:S(2)}, u32[]{:S(2)}) %all-to-all-start.5) | async-done | bytes 65568 | tf_op jit(solution)/shard_map/all_to_all | solution.py:190
  97.7 3.3 %all-to-all-start.6 = ((bf16[4,2,2048]{2,1,0:T(2,128)(2,1)}), bf16[4,2,2048]{2,1,0:T(2,128)(2,1)S(1)}, u32[]{:S(2)}, u32[]{:S(2)}) async-start(bf16[4,2,2048]{2,1,0:T(2,128)(2,1)} %reshape.436), calls=%async_computation.6 | async-start | bytes 65536 | tf_op jit(solution)/shard_map/all_to_all | solution.py:185
  101.8 4.8 %all-to-all-done.6 = bf16[4,2,2048]{2,1,0:T(2,128)(2,1)S(1)} async-done(((bf16[4,2,2048]{2,1,0:T(2,128)(2,1)}), bf16[4,2,2048]{2,1,0:T(2,128)(2,1)S(1)}, u32[]{:S(2)}, u32[]{:S(2)}) %all-to-all-start.6) | async-done | bytes 32800 | tf_op jit(solution)/shard_map/all_to_all | solution.py:185
  119.7 2.5 %collective-permute-done.15 = f32[416,640]{1,0:T(8,128)} collective-permute-done((f32[416,640]{1,0:T(8,128)}, f32[416,640]{1,0:T(8,128)}, u32[]{:S(2)}, u32[]{:S(2)}) %collective-permute-start.15) | collective-permute-done | bytes 1064992 | tf_op jit(solution)/shard_map/ppermute | solution.py:116
  122.1 1.7 bitcast_add_fusion
  124.7 8.5 %collective-permute-done.16 = f32[208,640]{1,0:T(8,128)S(1)} collective-permute-done((f32[208,640]{1,0:T(8,128)S(1)}, f32[208,640]{1,0:T(8,128)S(1)}, u32[]{:S(2)}, u32[]{:S(2)}) %collective-permute-start.16) | collective-permute-done | bytes 532512 | tf_op jit(solution)/shard_map/ppermute | solution.py:116
  133.3 1.6 collective-permute-start.17
  134.9 4.9 %collective-permute-done.17 = f32[104,640]{1,0:T(8,128)S(1)} collective-permute-done((f32[104,640]{1,0:T(8,128)S(1)}, f32[104,640]{1,0:T(8,128)S(1)}, u32[]{:S(2)}, u32[]{:S(2)}) %collective-permute-start.17) | collective-permute-done | bytes 266272 | tf_op jit(solution)/shard_map/ppermute | solution.py:116
  140.7 5.9 %collective-permute-done.18 = f32[104,640]{1,0:T(8,128)S(1)} collective-permute-done((f32[104,640]{1,0:T(8,128)S(1)}, f32[104,640]{1,0:T(8,128)S(1)}, u32[]{:S(2)}, u32[]{:S(2)}) %collective-permute-start.18) | collective-permute-done | bytes 266272 | tf_op jit(solution)/shard_map/ppermute | solution.py:116
  147.7 11.4 %collective-permute-done.19 = f32[104,640]{1,0:T(8,128)S(1)} collective-permute-done((f32[104,640]{1,0:T(8,128)S(1)}, f32[104,640]{1,0:T(8,128)S(1)}, u32[]{:S(2)}, u32[]{:S(2)}) %collective-permute-start.19) | collective-permute-done | bytes 266272 | tf_op jit(solution)/shard_map/ppermute | solution.py:116
  161.2 4.6 %collective-permute-done.20 = f32[104,640]{1,0:T(8,128)S(1)} collective-permute-done((f32[104,640]{1,0:T(8,128)S(1)}, f32[104,640]{1,0:T(8,128)S(1)}, u32[]{:S(2)}, u32[]{:S(2)}) %collective-permute-start.20) | collective-permute-done | bytes 266272 | tf_op jit(solution)/shard_map/ppermute | solution.py:116
  169.8 5.4 %collective-permute-done.21 = f32[208,640]{1,0:T(8,128)S(1)} collective-permute-done((f32[208,640]{1,0:T(8,128)S(1)}, f32[208,640]{1,0:T(8,128)S(1)}, u32[]{:S(2)}, u32[]{:S(2)}) %collective-permute-start.21) | collective-permute-done | bytes 532512 | tf_op jit(solution)/shard_map/ppermute | solution.py:116
  178.3 3.3 %all-to-all-start.7 = ((f32[2,32,256]{2,0,1:T(2,128)}), f32[2,32,256]{2,0,1:T(2,128)S(1)}, u32[]{:S(2)}, u32[]{:S(2)}) async-start(f32[2,32,256]{2,0,1:T(2,128)} %copy.182), calls=%async_computation.7 | async-start | bytes 131072 | tf_op jit(solution)/shard_map/all_to_all | solution.py:190
  183.3 4.0 %all-to-all-done.7 = f32[2,32,256]{2,0,1:T(2,128)S(1)} async-done(((f32[2,32,256]{2,0,1:T(2,128)}), f32[2,32,256]{2,0,1:T(2,128)S(1)}, u32[]{:S(2)}, u32[]{:S(2)}) %all-to-all-start.7) | async-done | bytes 65568 | tf_op jit(solution)/shard_map/all_to_all | solution.py:190
  (252 shorter events, 63.4 us)
Async XLA Ops:
  0.6 23.6 %copy-start = (bf16[640,640]{1,0:T(8,128)(2,1)S(1)}, bf16[640,640]{1,0:T(8,128)(2,1)}, u32[]{:S(2)}) copy-start(bf16[640,640]{1,0:T(8,128)(2,1)} %param.22) | copy-start | bytes 2457604
  1.7 18.1 %collective-permute-start.4 = (f32[1,1,2,32]{3,2,1,0:T(2,128)S(1)}, f32[1,1,2,32]{3,2,1,0:T(2,128)S(1)}, u32[]{:S(2)}, u32[]{:S(2)}) collective-permute-start(f32[1,1,2,32]{3,2,1,0:T(2,128)S(1)} %maximum_bitcast_fusion.4), channel_id=1, source_target_pairs={{4,0},{8,4},{12,8},{16,12},{20,16},{24,20},{28,24},{0,28},{5,1},{9... | collective-permute-start | bytes 776 | tf_op jit(solution)/shard_map/ppermute | solution.py:24
  5.1 12.8 %collective-permute-start.3 = (f32[1,1,2,32]{3,2,1,0:T(2,128)S(1)}, f32[1,1,2,32]{3,2,1,0:T(2,128)S(1)}, u32[]{:S(2)}, u32[]{:S(2)}) collective-permute-start(f32[1,1,2,32]{3,2,1,0:T(2,128)S(1)} %maximum_bitcast_fusion.4), channel_id=1, source_target_pairs={{0,4},{4,8},{8,12},{12,16},{16,20},{20,24},{24,28},{28,0},{1,5},{5... | collective-permute-start | bytes 776 | tf_op jit(solution)/shard_map/ppermute | solution.py:22
  6.5 15.3 %collective-permute-start.1 = (f32[1,16,2,32]{3,1,2,0:T(8,128)S(1)}, f32[1,16,2,32]{3,1,2,0:T(8,128)S(1)}, u32[]{:S(2)}, u32[]{:S(2)}) collective-permute-start(f32[1,16,2,32]{3,1,2,0:T(8,128)S(1)} %maximum_bitcast_fusion), channel_id=1, source_target_pairs={{4,0},{8,4},{12,8},{16,12},{20,16},{24,20},{28,24},{0,28},{5,1},{9... | collective-permute-start | bytes 12296 | tf_op jit(solution)/shard_map/ppermute | solution.py:24
  9.2 12.6 %collective-permute-start = (f32[1,16,2,32]{3,1,2,0:T(8,128)S(1)}, f32[1,16,2,32]{3,1,2,0:T(8,128)S(1)}, u32[]{:S(2)}, u32[]{:S(2)}) collective-permute-start(f32[1,16,2,32]{3,1,2,0:T(8,128)S(1)} %maximum_bitcast_fusion), channel_id=1, source_target_pairs={{0,4},{4,8},{8,12},{12,16},{16,20},{20,24},{24,28},{28,0},{1,5},{5... | collective-permute-start | bytes 12296 | tf_op jit(solution)/shard_map/ppermute | solution.py:22
  9.2 10.3 %collective-permute-start.5 = (f32[1,2,32]{2,1,0:T(2,128)S(1)}, f32[1,2,32]{2,1,0:T(2,128)S(1)}, u32[]{:S(2)}, u32[]{:S(2)}) collective-permute-start(f32[1,2,32]{2,1,0:T(2,128)S(1)} %pad_maximum_fusion.4), channel_id=1, source_target_pairs={{0,16},{4,20},{8,24},{12,28},{16,0},{20,4},{24,8},{28,12},{1,17},{... | collective-permute-start | bytes 776 | tf_op jit(solution)/shard_map/ppermute | solution.py:33
  12.1 10.5 %all-to-all-start = ((bf16[4,2,2048]{2,1,0:T(2,128)(2,1)}), bf16[4,2,2048]{2,1,0:T(2,128)(2,1)S(1)}, u32[]{:S(2)}, u32[]{:S(2)}) async-start(bf16[4,2,2048]{2,1,0:T(2,128)(2,1)} %reshape.430), calls=%async_computation | async-start | bytes 65536 | tf_op jit(solution)/shard_map/all_to_all | solution.py:185
  17.9 3.8 %collective-permute-start.2 = (f32[16,2,32]{2,1,0:T(2,128)S(1)}, f32[16,2,32]{2,1,0:T(2,128)S(1)}, u32[]{:S(2)}, u32[]{:S(2)}) collective-permute-start(f32[16,2,32]{2,1,0:T(2,128)S(1)} %pad_maximum_fusion), channel_id=1, source_target_pairs={{0,16},{4,20},{8,24},{12,28},{16,0},{20,4},{24,8},{28,12},{1,17},{... | collective-permute-start | bytes 12296 | tf_op jit(solution)/shard_map/ppermute | solution.py:33
  27.3 10.6 %all-to-all-start.1 = ((f32[2,32,256]{2,0,1:T(2,128)}), f32[2,32,256]{2,0,1:T(2,128)S(1)}, u32[]{:S(2)}, u32[]{:S(2)}) async-start(f32[2,32,256]{2,0,1:T(2,128)} %copy.161), calls=%async_computation.1 | async-start | bytes 131072 | tf_op jit(solution)/shard_map/all_to_all | solution.py:190
  38.4 7.8 %collective-permute-start.7 = (f32[1,16,2,32]{3,1,2,0:T(8,128)S(1)}, f32[1,16,2,32]{3,1,2,0:T(8,128)S(1)}, u32[]{:S(2)}, u32[]{:S(2)}) collective-permute-start(f32[1,16,2,32]{3,1,2,0:T(8,128)S(1)} %maximum_bitcast_fusion.1), channel_id=1, source_target_pairs={{4,0},{8,4},{12,8},{16,12},{20,16},{24,20},{28,24},{0,28},{5,1},{9... | collective-permute-start | bytes 12296 | tf_op jit(solution)/shard_map/ppermute | solution.py:24
  38.5 7.8 %collective-permute-start.6 = (f32[1,16,2,32]{3,1,2,0:T(8,128)S(1)}, f32[1,16,2,32]{3,1,2,0:T(8,128)S(1)}, u32[]{:S(2)}, u32[]{:S(2)}) collective-permute-start(f32[1,16,2,32]{3,1,2,0:T(8,128)S(1)} %maximum_bitcast_fusion.1), channel_id=1, source_target_pairs={{0,4},{4,8},{8,12},{12,16},{16,20},{20,24},{24,28},{28,0},{1,5},{5... | collective-permute-start | bytes 12296 | tf_op jit(solution)/shard_map/ppermute | solution.py:22
  39.2 7.1 %collective-permute-start.8 = (f32[16,2,32]{2,1,0:T(2,128)S(1)}, f32[16,2,32]{2,1,0:T(2,128)S(1)}, u32[]{:S(2)}, u32[]{:S(2)}) collective-permute-start(f32[16,2,32]{2,1,0:T(2,128)S(1)} %pad_maximum_fusion.1), channel_id=1, source_target_pairs={{0,16},{4,20},{8,24},{12,28},{16,0},{20,4},{24,8},{28,12},{1,17},{... | collective-permute-start | bytes 12296 | tf_op jit(solution)/shard_map/ppermute | solution.py:33
  43.0 8.9 %all-to-all-start.2 = ((bf16[4,2,2048]{2,1,0:T(2,128)(2,1)}), bf16[4,2,2048]{2,1,0:T(2,128)(2,1)S(1)}, u32[]{:S(2)}, u32[]{:S(2)}) async-start(bf16[4,2,2048]{2,1,0:T(2,128)(2,1)} %reshape.432), calls=%async_computation.2 | async-start | bytes 65536 | tf_op jit(solution)/shard_map/all_to_all | solution.py:185
  56.4 9.7 %all-to-all-start.3 = ((f32[2,32,256]{2,0,1:T(2,128)}), f32[2,32,256]{2,0,1:T(2,128)}, u32[]{:S(2)}, u32[]{:S(2)}) async-start(f32[2,32,256]{2,0,1:T(2,128)} %copy.168), calls=%async_computation.3 | async-start | bytes 131072 | tf_op jit(solution)/shard_map/all_to_all | solution.py:190
  69.0 6.7 %collective-permute-start.10 = (f32[1,16,2,32]{3,1,2,0:T(8,128)S(1)}, f32[1,16,2,32]{3,1,2,0:T(8,128)S(1)}, u32[]{:S(2)}, u32[]{:S(2)}) collective-permute-start(f32[1,16,2,32]{3,1,2,0:T(8,128)S(1)} %maximum_bitcast_fusion.2), channel_id=1, source_target_pairs={{4,0},{8,4},{12,8},{16,12},{20,16},{24,20},{28,24},{0,28},{5,1},{9... | collective-permute-start | bytes 12296 | tf_op jit(solution)/shard_map/ppermute | solution.py:24
  69.1 6.2 %collective-permute-start.9 = (f32[1,16,2,32]{3,1,2,0:T(8,128)S(1)}, f32[1,16,2,32]{3,1,2,0:T(8,128)S(1)}, u32[]{:S(2)}, u32[]{:S(2)}) collective-permute-start(f32[1,16,2,32]{3,1,2,0:T(8,128)S(1)} %maximum_bitcast_fusion.2), channel_id=1, source_target_pairs={{0,4},{4,8},{8,12},{12,16},{16,20},{20,24},{24,28},{28,0},{1,5},{5... | collective-permute-start | bytes 12296 | tf_op jit(solution)/shard_map/ppermute | solution.py:22
  69.7 5.5 %collective-permute-start.11 = (f32[16,2,32]{2,1,0:T(2,128)S(1)}, f32[16,2,32]{2,1,0:T(2,128)S(1)}, u32[]{:S(2)}, u32[]{:S(2)}) collective-permute-start(f32[16,2,32]{2,1,0:T(2,128)S(1)} %pad_maximum_fusion.2), channel_id=1, source_target_pairs={{0,16},{4,20},{8,24},{12,28},{16,0},{20,4},{24,8},{28,12},{1,17},{... | collective-permute-start | bytes 12296 | tf_op jit(solution)/shard_map/ppermute | solution.py:33
  71.9 9.0 %all-to-all-start.4 = ((bf16[4,2,2048]{2,1,0:T(2,128)(2,1)}), bf16[4,2,2048]{2,1,0:T(2,128)(2,1)S(1)}, u32[]{:S(2)}, u32[]{:S(2)}) async-start(bf16[4,2,2048]{2,1,0:T(2,128)(2,1)} %reshape.434), calls=%async_computation.4 | async-start | bytes 65536 | tf_op jit(solution)/shard_map/all_to_all | solution.py:185
  86.5 9.0 %all-to-all-start.5 = ((f32[2,32,256]{2,0,1:T(2,128)}), f32[2,32,256]{2,0,1:T(2,128)S(1)}, u32[]{:S(2)}, u32[]{:S(2)}) async-start(f32[2,32,256]{2,0,1:T(2,128)} %copy.175), calls=%async_computation.5 | async-start | bytes 131072 | tf_op jit(solution)/shard_map/all_to_all | solution.py:190
  97.7 8.9 %all-to-all-start.6 = ((bf16[4,2,2048]{2,1,0:T(2,128)(2,1)}), bf16[4,2,2048]{2,1,0:T(2,128)(2,1)S(1)}, u32[]{:S(2)}, u32[]{:S(2)}) async-start(bf16[4,2,2048]{2,1,0:T(2,128)(2,1)} %reshape.436), calls=%async_computation.6 | async-start | bytes 65536 | tf_op jit(solution)/shard_map/all_to_all | solution.py:185
  119.1 3.0 %collective-permute-start.15 = (f32[416,640]{1,0:T(8,128)}, f32[416,640]{1,0:T(8,128)}, u32[]{:S(2)}, u32[]{:S(2)}) collective-permute-start(f32[416,640]{1,0:T(8,128)} %dynamic-slice_bitcast_fusion), channel_id=1, source_target_pairs={{0,4},{4,0},{8,12},{12,8},{16,20},{20,16},{24,28},{28,24},{1,5},{5... | collective-permute-start | bytes 3194888 | tf_op jit(solution)/shard_map/ppermute | solution.py:116
  123.8 9.3 %collective-permute-start.16 = (f32[208,640]{1,0:T(8,128)S(1)}, f32[208,640]{1,0:T(8,128)S(1)}, u32[]{:S(2)}, u32[]{:S(2)}) collective-permute-start(f32[208,640]{1,0:T(8,128)S(1)} %dynamic-slice_bitcast_fusion.1), channel_id=1, source_target_pairs={{0,8},{4,20},{8,0},{12,28},{16,24},{20,4},{24,16},{28,12},{1,9},{5... | collective-permute-start | bytes 1597448 | tf_op jit(solution)/shard_map/ppermute | solution.py:116
  133.3 6.5 %collective-permute-start.17 = (f32[104,640]{1,0:T(8,128)S(1)}, f32[104,640]{1,0:T(8,128)S(1)}, u32[]{:S(2)}, u32[]{:S(2)}) collective-permute-start(f32[104,640]{1,0:T(8,128)S(1)} %dynamic-slice_bitcast_fusion.2), channel_id=1, source_target_pairs={{0,16},{4,12},{8,24},{12,4},{16,0},{20,28},{24,8},{28,20},{1,17},{... | collective-permute-start | bytes 798728 | tf_op jit(solution)/shard_map/ppermute | solution.py:116
  139.8 6.8 %collective-permute-start.18 = (f32[104,640]{1,0:T(8,128)S(1)}, f32[104,640]{1,0:T(8,128)S(1)}, u32[]{:S(2)}, u32[]{:S(2)}) collective-permute-start(f32[104,640]{1,0:T(8,128)S(1)} %bitcast_add_fusion.2), channel_id=1, source_target_pairs={{0,1},{1,0},{2,3},{3,2},{4,5},{5,4},{6,7},{7,6},{8,9},{9,8},{10,11... | collective-permute-start | bytes 798728 | tf_op jit(solution)/shard_map/ppermute | solution.py:116
  146.6 12.5 %collective-permute-start.19 = (f32[104,640]{1,0:T(8,128)S(1)}, f32[104,640]{1,0:T(8,128)S(1)}, u32[]{:S(2)}, u32[]{:S(2)}) collective-permute-start(f32[104,640]{1,0:T(8,128)S(1)} %add.383), channel_id=1, source_target_pairs={{0,2},{1,3},{2,0},{3,1},{4,6},{5,7},{6,4},{7,5},{8,10},{9,11},{10,... | collective-permute-start | bytes 798728 | tf_op jit(solution)/shard_map/ppermute | solution.py:116
  159.1 6.7 %collective-permute-start.20 = (f32[104,640]{1,0:T(8,128)S(1)}, f32[104,640]{1,0:T(8,128)S(1)}, u32[]{:S(2)}, u32[]{:S(2)}) collective-permute-start(f32[104,640]{1,0:T(8,128)S(1)} %add.384), channel_id=1, source_target_pairs={{0,16},{4,12},{8,24},{12,4},{16,0},{20,28},{24,8},{28,20},{1,17},{... | collective-permute-start | bytes 798728 | tf_op jit(solution)/shard_map/ppermute | solution.py:116
  160.7 15.8 %collective-permute-start.13 = (f32[1,16,2,32]{3,1,2,0:T(8,128)S(1)}, f32[1,16,2,32]{3,1,2,0:T(8,128)S(1)}, u32[]{:S(2)}, u32[]{:S(2)}) collective-permute-start(f32[1,16,2,32]{3,1,2,0:T(8,128)S(1)} %maximum_bitcast_fusion.3), channel_id=1, source_target_pairs={{4,0},{8,4},{12,8},{16,12},{20,16},{24,20},{28,24},{0,28},{5,1},{9... | collective-permute-start | bytes 12296 | tf_op jit(solution)/shard_map/ppermute | solution.py:24
  160.9 14.4 %collective-permute-start.12 = (f32[1,16,2,32]{3,1,2,0:T(8,128)S(1)}, f32[1,16,2,32]{3,1,2,0:T(8,128)S(1)}, u32[]{:S(2)}, u32[]{:S(2)}) collective-permute-start(f32[1,16,2,32]{3,1,2,0:T(8,128)S(1)} %maximum_bitcast_fusion.3), channel_id=1, source_target_pairs={{0,4},{4,8},{8,12},{12,16},{16,20},{20,24},{24,28},{28,0},{1,5},{5... | collective-permute-start | bytes 12296 | tf_op jit(solution)/shard_map/ppermute | solution.py:22
  165.8 9.3 %collective-permute-start.21 = (f32[208,640]{1,0:T(8,128)S(1)}, f32[208,640]{1,0:T(8,128)S(1)}, u32[]{:S(2)}, u32[]{:S(2)}) collective-permute-start(f32[208,640]{1,0:T(8,128)S(1)} %bitcast.194), channel_id=1, source_target_pairs={{0,8},{4,20},{8,0},{12,28},{16,24},{20,4},{24,16},{28,12},{1,9},{5... | collective-permute-start | bytes 1597448 | tf_op jit(solution)/shard_map/ppermute | solution.py:116
  166.7 8.6 %collective-permute-start.14 = (f32[16,2,32]{2,1,0:T(2,128)S(1)}, f32[16,2,32]{2,1,0:T(2,128)S(1)}, u32[]{:S(2)}, u32[]{:S(2)}) collective-permute-start(f32[16,2,32]{2,1,0:T(2,128)S(1)} %pad_maximum_fusion.3), channel_id=1, source_target_pairs={{0,16},{4,20},{8,24},{12,28},{16,0},{20,4},{24,8},{28,12},{1,17},{... | collective-permute-start | bytes 12296 | tf_op jit(solution)/shard_map/ppermute | solution.py:33
  175.3 12.8 %collective-permute-start.22 = (f32[416,640]{1,0:T(8,128)S(1)}, f32[416,640]{1,0:T(8,128)S(1)}, u32[]{:S(2)}, u32[]{:S(2)}) collective-permute-start(f32[416,640]{1,0:T(8,128)S(1)} %bitcast.190), channel_id=1, source_target_pairs={{0,4},{4,0},{8,12},{12,8},{16,20},{20,16},{24,28},{28,24},{1,5},{5... | collective-permute-start | bytes 3194888 | tf_op jit(solution)/shard_map/ppermute | solution.py:116
  178.3 9.0 %all-to-all-start.7 = ((f32[2,32,256]{2,0,1:T(2,128)}), f32[2,32,256]{2,0,1:T(2,128)S(1)}, u32[]{:S(2)}, u32[]{:S(2)}) async-start(f32[2,32,256]{2,0,1:T(2,128)} %copy.182), calls=%async_computation.7 | async-start | bytes 131072 | tf_op jit(solution)/shard_map/all_to_all | solution.py:190
  (27 other events, 172.8 us)
where the time goes:
time: 193 us; the launch traced here: 191 us
  waiting for transfers between devices  77.9 us (40%)
  starting transfers between devices  49.9 us (26%)
  local copies, waits for them, and re-layouts  32.4 us (17%)
  matrix products  15.8 us (8%)
  other arithmetic  13.6 us (7%)
    ppermute x8, waiting for transfers between devices, swapped(): lax.ppermute(x, axis, [(i, i ^ (odd_bit if i & 1 else even_bit)) for i in...  43.1 us
    all_to_all x4, waiting for transfers between devices, to_segments(): lax.all_to_all(shaped, 'depth', split_axis=1, concat_axis=2, tiled=True)  19.7 us
    all_to_all x4, starting transfers between devices, to_segments(): lax.all_to_all(shaped, 'depth', split_axis=1, concat_axis=2, tiled=True)  15.3 us
    all_to_all x4, starting transfers between devices, to_columns(): lax.all_to_all(segment, 'depth', split_axis=2, concat_axis=1, tiled=True)  14.8 us
    all_to_all x4, waiting for transfers between devices, to_columns(): lax.all_to_all(segment, 'depth', split_axis=2, concat_axis=1, tiled=True)  13.4 us
    unnamed x65, local copies, waits for them, and re-layouts  9.16 us
    ppermute x8, starting transfers between devices, swapped(): lax.ppermute(x, axis, [(i, i ^ (odd_bit if i & 1 else even_bit)) for i in...  6.47 us
    ppermute x5, starting transfers between devices, with_halo(): lax.ppermute(head, axis, [((i + 1) % count, i) for i in range(count)])  6.4 us
  transfers between devices with their start and end apart: 31, of which 16 were waited for; matrix products, arithmetic and copies ran while one was open for 12% of the time, Pallas kernels for 0%

commit v1 on v0

--- a/solution.py
+++ b/solution.py
@@ -187,7 +187,20 @@
 
     def to_segments(values):
         shaped = values.reshape(2, LEVELS, values.shape[1])
-        segment_part = lax.all_to_all(shaped, "depth", split_axis=1, concat_axis=2, tiled=True)
+        ways, here = (lax.axis_size("depth"), lax.axis_index("depth"))
+        width_2 = shaped.shape[1] // ways
+        dims = list(shaped.shape)
+        dims[1] = width_2
+        height = dims[2]
+        dims[2] = height * ways
+        segment_part = jnp.zeros(dims, shaped.dtype)
+        for mask in range(ways):
+            part_2 = lax.dynamic_slice_in_dim(shaped, (here ^ mask) * width_2, width_2, axis=1)
+            if mask:
+                part_2 = lax.ppermute(part_2, "depth", [(d, d ^ mask) for d in range(ways)])
+            segment_part = lax.dynamic_update_slice_in_dim(
+                segment_part, part_2, (here ^ mask) * height, axis=2
+            )
         return segment_part
 
     state_now = initial_state

time: 193 us -> 185 us (0.959)
  waiting for transfers between devices: 77.9 us -> 68.9 us
  starting transfers between devices: 49.9 us -> 52.4 us
    all_to_all x4 -> x0, waiting for transfers between devices: 19.7 us -> none  [to_segments(): lax.all_to_all(shaped, 'depth', split_axis=1, concat_axis=2, tiled=True)]
    all_to_all x4 -> x0, starting transfers between devices: 15.3 us -> none  [to_segments(): lax.all_to_all(shaped, 'depth', split_axis=1, concat_axis=2, tiled=True)]
    ppermute x0 -> x12, starting transfers between devices: none -> 15.1 us  [to_segments(): part_2 = lax.ppermute(part_2, 'depth', [(d, d ^ mask) for d in range(ways)])]
    ppermute x0 -> x12, waiting for transfers between devices: none -> 12.4 us  [to_segments(): part_2 = lax.ppermute(part_2, 'depth', [(d, d ^ mask) for d in range(ways)])]
    ppermute x8, waiting for transfers between devices: 43.1 us -> 38.8 us  [swapped(): lax.ppermute(x, axis, [(i, i ^ (odd_bit if i & 1 else even_bit)) for i in...]
    reshape x4 -> x0, local copies, waits for them, and re-layouts: 2.76 us -> none  [to_segments(): shaped = values.reshape(2, LEVELS, values.shape[1])]
    dynamic_update_slice x0 -> x12, local copies, waits for them, and re-layouts: none -> 2.56 us  [to_segments(): lax.dynamic_update_slice_in_dim(segment_part, part_2, (here ^ mask) * hei...]
    ppermute x5, waiting for transfers between devices: 1.68 us -> 4.18 us  [passed_along(): lax.ppermute(x, axis, [(i, (i + by) % length) for i in range(length)])]
  transfers between devices with their start and end apart: 31 -> 39, of which waited for: 16 -> 19; matrix products, arithmetic and copies ran while one was open for 12% -> 13% of each run, Pallas kernels for 0% -> 0%
where the time goes in v1:
time: 185 us; the launch traced here: 184 us
  waiting for transfers between devices  68.9 us (37%)
  starting transfers between devices  52.4 us (28%)
  local copies, waits for them, and re-layouts  32 us (17%)
  matrix products  15.9 us (9%)
  other arithmetic  13 us (7%)
    ppermute x8, waiting for transfers between devices, swapped(): lax.ppermute(x, axis, [(i, i ^ (odd_bit if i & 1 else even_bit)) for i in...  38.8 us
    all_to_all x4, starting transfers between devices, to_columns(): lax.all_to_all(segment, 'depth', split_axis=2, concat_axis=1, tiled=True)  15.7 us
    ppermute x12, starting transfers between devices, to_segments(): part_2 = lax.ppermute(part_2, 'depth', [(d, d ^ mask) for d in range(ways)])  15.1 us
    all_to_all x4, waiting for transfers between devices, to_columns(): lax.all_to_all(segment, 'depth', split_axis=2, concat_axis=1, tiled=True)  13.5 us
    ppermute x12, waiting for transfers between devices, to_segments(): part_2 = lax.ppermute(part_2, 'depth', [(d, d ^ mask) for d in range(ways)])  12.4 us
    unnamed x71, local copies, waits for them, and re-layouts  9.15 us
    ppermute x5, starting transfers between devices, with_halo(): lax.ppermute(head, axis, [((i + 1) % count, i) for i in range(count)])  8.88 us
    ppermute x8, starting transfers between devices, swapped(): lax.ppermute(x, axis, [(i, i ^ (odd_bit if i & 1 else even_bit)) for i in...  5.86 us
  transfers between devices with their start and end apart: 39, of which 19 were waited for; matrix products, arithmetic and copies ran while one was open for 13% of the time, Pallas kernels for 0%

profile of v1, /device:TPU:0, one launch (start us, length us, event | category | flops | bytes accessed | tf_op | source)
XLA Modules:
  0.0 184.0 jit_solution(15736894074795507236)
XLA Ops:
  1.7 3.4 %collective-permute-start.4 = (f32[1,1,2,32]{3,2,1,0:T(2,128)S(1)}, f32[1,1,2,32]{3,2,1,0:T(2,128)S(1)}, u32[]{:S(2)}, u32[]{:S(2)}) collective-permute-start(f32[1,1,2,32]{3,2,1,0:T(2,128)S(1)} %maximum_bitcast_fusion.4), channel_id=1, source_target_pairs={{4,0},{8,4},{12,8},{16,12},{20,16},{24,20},{28,24},{0,28},{5,1},{9... | collective-permute-start | bytes 776 | tf_op jit(solution)/shard_map/ppermute | solution.py:24
  6.5 2.7 %collective-permute-start.1 = (f32[1,16,2,32]{3,1,2,0:T(8,128)S(1)}, f32[1,16,2,32]{3,1,2,0:T(8,128)S(1)}, u32[]{:S(2)}, u32[]{:S(2)}) collective-permute-start(f32[1,16,2,32]{3,1,2,0:T(8,128)S(1)} %maximum_bitcast_fusion), channel_id=1, source_target_pairs={{4,0},{8,4},{12,8},{16,12},{20,16},{24,20},{28,24},{0,28},{5,1},{9... | collective-permute-start | bytes 12296 | tf_op jit(solution)/shard_map/ppermute | solution.py:24
  12.1 4.9 %all-to-all-start = ((bf16[4,2,2048]{2,1,0:T(2,128)(2,1)}), bf16[4,2,2048]{2,1,0:T(2,128)(2,1)S(1)}, u32[]{:S(2)}, u32[]{:S(2)}) async-start(bf16[4,2,2048]{2,1,0:T(2,128)(2,1)} %reshape.430), calls=%async_computation | async-start | bytes 65536 | tf_op jit(solution)/shard_map/all_to_all | solution.py:185
  18.0 1.6 collective-permute-start.2
  20.1 1.7 collective-permute-done.2
  24.3 2.1 %multiply_convert_fusion.2 = (bf16[640,256]{0,1:T(8,128)(2,1)S(1)}, f32[640,256]{0,1:T(8,128)}) fusion(f32[640]{0:T(1024)} %param.23, bf16[640,640]{1,0:T(8,128)(2,1)S(1)} %copy-done, f32[640,256]{0,1:T(8,128)S(1)} %convolution_add_fusion.3), kind=kOutput, calls=%fused_computation.40 | convolution fusion | flops 211517440 | bytes 2460160 | tf_op jit(solution)/shard_map/dot_general | solution.py:73
  26.7 1.9 %collective-permute-start.6 = (f32[2,8,256]{2,1,0:T(8,128)S(1)}, f32[2,8,256]{2,1,0:T(8,128)S(1)}, u32[]{:S(2)}, u32[]{:S(2)}) collective-permute-start(f32[2,8,256]{2,1,0:T(8,128)S(1)} %get-tuple-element.103), channel_id=1, source_target_pairs={{0,1},{1,0},{2,3},{3,2},{4,5},{5,4},{6,7},{7,6},{8,9},{9,8},{10,11... | collective-permute-start | bytes 49160 | tf_op jit(solution)/shard_map/ppermute | solution.py:200
  28.9 2.4 %collective-permute-start.8 = (f32[2,8,256]{2,1,0:T(8,128)S(1)}, f32[2,8,256]{2,1,0:T(8,128)S(1)}, u32[]{:S(2)}, u32[]{:S(2)}) collective-permute-start(f32[2,8,256]{2,1,0:T(8,128)S(1)} %get-tuple-element.101), channel_id=1, source_target_pairs={{0,3},{1,2},{2,1},{3,0},{4,7},{5,6},{6,5},{7,4},{8,11},{9,10},{10,... | collective-permute-start | bytes 49160 | tf_op jit(solution)/shard_map/ppermute | solution.py:200
  31.4 4.7 %collective-permute-done.7 = f32[2,8,256]{2,1,0:T(8,128)S(1)} collective-permute-done((f32[2,8,256]{2,1,0:T(8,128)S(1)}, f32[2,8,256]{2,1,0:T(8,128)S(1)}, u32[]{:S(2)}, u32[]{:S(2)}) %collective-permute-start.7) | collective-permute-done | bytes 16416 | tf_op jit(solution)/shard_map/ppermute | solution.py:200
  41.2 3.3 %all-to-all-start.1 = ((bf16[4,2,2048]{2,1,0:T(2,128)(2,1)}), bf16[4,2,2048]{2,1,0:T(2,128)(2,1)S(1)}, u32[]{:S(2)}, u32[]{:S(2)}) async-start(bf16[4,2,2048]{2,1,0:T(2,128)(2,1)} %reshape.432), calls=%async_computation.1 | async-start | bytes 65536 | tf_op jit(solution)/shard_map/all_to_all | solution.py:185
  46.4 3.8 %all-to-all-done.1 = bf16[4,2,2048]{2,1,0:T(2,128)(2,1)S(1)} async-done(((bf16[4,2,2048]{2,1,0:T(2,128)(2,1)}), bf16[4,2,2048]{2,1,0:T(2,128)(2,1)S(1)}, u32[]{:S(2)}, u32[]{:S(2)}) %all-to-all-start.1) | async-done | bytes 32800 | tf_op jit(solution)/shard_map/all_to_all | solution.py:185
  51.5 2.3 %multiply_convert_fusion = (bf16[640,256]{0,1:T(8,128)(2,1)S(1)}, f32[640,256]{0,1:T(8,128)}) fusion(f32[640]{0:T(1024)} %param.23, bf16[640,640]{1,0:T(8,128)(2,1)S(1)} %copy-done, f32[640,256]{0,1:T(8,128)S(1)} %fusion.3), kind=kOutput, calls=%fused_computation.36 | convolution fusion | flops 211517440 | bytes 2460160 | tf_op jit(solution)/shard_map/dot_general | solution.py:73
  60.1 2.0 %collective-permute-done.13 = f32[2,8,256]{2,1,0:T(8,128)S(1)} collective-permute-done((f32[2,8,256]{2,1,0:T(8,128)}, f32[2,8,256]{2,1,0:T(8,128)S(1)}, u32[]{:S(2)}, u32[]{:S(2)}) %collective-permute-start.13) | collective-permute-done | bytes 16416 | tf_op jit(solution)/shard_map/ppermute | solution.py:200
  68.2 3.9 %all-to-all-start.2 = ((bf16[4,2,2048]{2,1,0:T(2,128)(2,1)}), bf16[4,2,2048]{2,1,0:T(2,128)(2,1)S(1)}, u32[]{:S(2)}, u32[]{:S(2)}) async-start(bf16[4,2,2048]{2,1,0:T(2,128)(2,1)} %reshape.434), calls=%async_computation.2 | async-start | bytes 65536 | tf_op jit(solution)/shard_map/all_to_all | solution.py:185
  73.1 4.7 %all-to-all-done.2 = bf16[4,2,2048]{2,1,0:T(2,128)(2,1)S(1)} async-done(((bf16[4,2,2048]{2,1,0:T(2,128)(2,1)}), bf16[4,2,2048]{2,1,0:T(2,128)(2,1)S(1)}, u32[]{:S(2)}, u32[]{:S(2)}) %all-to-all-start.2) | async-done | bytes 32800 | tf_op jit(solution)/shard_map/all_to_all | solution.py:185
  80.8 1.7 fusion.28
  86.6 3.2 %collective-permute-done.19 = f32[2,8,256]{2,1,0:T(8,128)S(1)} collective-permute-done((f32[2,8,256]{2,1,0:T(8,128)S(1)}, f32[2,8,256]{2,1,0:T(8,128)S(1)}, u32[]{:S(2)}, u32[]{:S(2)}) %collective-permute-start.19) | collective-permute-done | bytes 16416 | tf_op jit(solution)/shard_map/ppermute | solution.py:200
  92.0 3.7 %all-to-all-start.3 = ((bf16[4,2,2048]{2,1,0:T(2,128)(2,1)}), bf16[4,2,2048]{2,1,0:T(2,128)(2,1)S(1)}, u32[]{:S(2)}, u32[]{:S(2)}) async-start(bf16[4,2,2048]{2,1,0:T(2,128)(2,1)} %reshape.436), calls=%async_computation.3 | async-start | bytes 65536 | tf_op jit(solution)/shard_map/all_to_all | solution.py:185
  96.6 4.8 %all-to-all-done.3 = bf16[4,2,2048]{2,1,0:T(2,128)(2,1)S(1)} async-done(((bf16[4,2,2048]{2,1,0:T(2,128)(2,1)}), bf16[4,2,2048]{2,1,0:T(2,128)(2,1)S(1)}, u32[]{:S(2)}, u32[]{:S(2)}) %all-to-all-start.3) | async-done | bytes 32800 | tf_op jit(solution)/shard_map/all_to_all | solution.py:185
  114.4 2.5 %collective-permute-done.27 = f32[416,640]{1,0:T(8,128)} collective-permute-done((f32[416,640]{1,0:T(8,128)}, f32[416,640]{1,0:T(8,128)}, u32[]{:S(2)}, u32[]{:S(2)}) %collective-permute-start.27) | collective-permute-done | bytes 1064992 | tf_op jit(solution)/shard_map/ppermute | solution.py:116
  116.9 1.7 bitcast_add_fusion
  119.3 8.7 %collective-permute-done.28 = f32[208,640]{1,0:T(8,128)S(1)} collective-permute-done((f32[208,640]{1,0:T(8,128)S(1)}, f32[208,640]{1,0:T(8,128)S(1)}, u32[]{:S(2)}, u32[]{:S(2)}) %collective-permute-start.28) | collective-permute-done | bytes 532512 | tf_op jit(solution)/shard_map/ppermute | solution.py:116
  128.1 1.6 collective-permute-start.29
  129.8 4.8 %collective-permute-done.29 = f32[104,640]{1,0:T(8,128)S(1)} collective-permute-done((f32[104,640]{1,0:T(8,128)S(1)}, f32[104,640]{1,0:T(8,128)S(1)}, u32[]{:S(2)}, u32[]{:S(2)}) %collective-permute-start.29) | collective-permute-done | bytes 266272 | tf_op jit(solution)/shard_map/ppermute | solution.py:116
  135.4 6.0 %collective-permute-done.30 = f32[104,640]{1,0:T(8,128)S(1)} collective-permute-done((f32[104,640]{1,0:T(8,128)S(1)}, f32[104,640]{1,0:T(8,128)S(1)}, u32[]{:S(2)}, u32[]{:S(2)}) %collective-permute-start.30) | collective-permute-done | bytes 266272 | tf_op jit(solution)/shard_map/ppermute | solution.py:116
  143.3 10.6 %collective-permute-done.31 = f32[104,640]{1,0:T(8,128)S(1)} collective-permute-done((f32[104,640]{1,0:T(8,128)S(1)}, f32[104,640]{1,0:T(8,128)S(1)}, u32[]{:S(2)}, u32[]{:S(2)}) %collective-permute-start.31) | collective-permute-done | bytes 266272 | tf_op jit(solution)/shard_map/ppermute | solution.py:116
  155.5 2.6 %collective-permute-start.22 = (f32[1,16,2,32]{3,1,2,0:T(8,128)S(1)}, f32[1,16,2,32]{3,1,2,0:T(8,128)S(1)}, u32[]{:S(2)}, u32[]{:S(2)}) collective-permute-start(f32[1,16,2,32]{3,1,2,0:T(8,128)S(1)} %maximum_bitcast_fusion.3), channel_id=1, source_target_pairs={{4,0},{8,4},{12,8},{16,12},{20,16},{24,20},{28,24},{0,28},{5,1},{9... | collective-permute-start | bytes 12296 | tf_op jit(solution)/shard_map/ppermute | solution.py:24
  159.0 1.6 collective-permute-done.32
  162.7 2.5 %collective-permute-done.23 = f32[16,2,32]{2,1,0:T(2,128)S(1)} collective-permute-done((f32[16,2,32]{2,1,0:T(2,128)S(1)}, f32[16,2,32]{2,1,0:T(2,128)S(1)}, u32[]{:S(2)}, u32[]{:S(2)}) %collective-permute-start.23) | collective-permute-done | bytes 4128 | tf_op jit(solution)/shard_map/ppermute | solution.py:33
  165.2 4.8 %collective-permute-done.33 = f32[208,640]{1,0:T(8,128)S(1)} collective-permute-done((f32[208,640]{1,0:T(8,128)S(1)}, f32[208,640]{1,0:T(8,128)S(1)}, u32[]{:S(2)}, u32[]{:S(2)}) %collective-permute-start.33) | collective-permute-done | bytes 532512 | tf_op jit(solution)/shard_map/ppermute | solution.py:116
  175.3 2.5 %collective-permute-start.25 = (f32[2,8,256]{2,1,0:T(8,128)S(1)}, f32[2,8,256]{2,1,0:T(8,128)S(1)}, u32[]{:S(2)}, u32[]{:S(2)}) collective-permute-start(f32[2,8,256]{2,1,0:T(8,128)S(1)} %get-tuple-element.90), channel_id=1, source_target_pairs={{0,2},{1,3},{2,0},{3,1},{4,6},{5,7},{6,4},{7,5},{8,10},{9,11},{10,... | collective-permute-start | bytes 49160 | tf_op jit(solution)/shard_map/ppermute | solution.py:200
  177.8 2.3 %collective-permute-done.25 = f32[2,8,256]{2,1,0:T(8,128)S(1)} collective-permute-done((f32[2,8,256]{2,1,0:T(8,128)S(1)}, f32[2,8,256]{2,1,0:T(8,128)S(1)}, u32[]{:S(2)}, u32[]{:S(2)}) %collective-permute-start.25) | collective-permute-done | bytes 16416 | tf_op jit(solution)/shard_map/ppermute | solution.py:200
  (286 shorter events, 71.7 us)
Async XLA Ops:
  1.7 18.1 %collective-permute-start.4 = (f32[1,1,2,32]{3,2,1,0:T(2,128)S(1)}, f32[1,1,2,32]{3,2,1,0:T(2,128)S(1)}, u32[]{:S(2)}, u32[]{:S(2)}) collective-permute-start(f32[1,1,2,32]{3,2,1,0:T(2,128)S(1)} %maximum_bitcast_fusion.4), channel_id=1, source_target_pairs={{4,0},{8,4},{12,8},{16,12},{20,16},{24,20},{28,24},{0,28},{5,1},{9... | collective-permute-start | bytes 776 | tf_op jit(solution)/shard_map/ppermute | solution.py:24
  5.1 12.9 %collective-permute-start.3 = (f32[1,1,2,32]{3,2,1,0:T(2,128)S(1)}, f32[1,1,2,32]{3,2,1,0:T(2,128)S(1)}, u32[]{:S(2)}, u32[]{:S(2)}) collective-permute-start(f32[1,1,2,32]{3,2,1,0:T(2,128)S(1)} %maximum_bitcast_fusion.4), channel_id=1, source_target_pairs={{0,4},{4,8},{8,12},{12,16},{16,20},{20,24},{24,28},{28,0},{1,5},{5... | collective-permute-start | bytes 776 | tf_op jit(solution)/shard_map/ppermute | solution.py:22
  6.5 15.3 %collective-permute-start.1 = (f32[1,16,2,32]{3,1,2,0:T(8,128)S(1)}, f32[1,16,2,32]{3,1,2,0:T(8,128)S(1)}, u32[]{:S(2)}, u32[]{:S(2)}) collective-permute-start(f32[1,16,2,32]{3,1,2,0:T(8,128)S(1)} %maximum_bitcast_fusion), channel_id=1, source_target_pairs={{4,0},{8,4},{12,8},{16,12},{20,16},{24,20},{28,24},{0,28},{5,1},{9... | collective-permute-start | bytes 12296 | tf_op jit(solution)/shard_map/ppermute | solution.py:24
  9.2 12.6 %collective-permute-start = (f32[1,16,2,32]{3,1,2,0:T(8,128)S(1)}, f32[1,16,2,32]{3,1,2,0:T(8,128)S(1)}, u32[]{:S(2)}, u32[]{:S(2)}) collective-permute-start(f32[1,16,2,32]{3,1,2,0:T(8,128)S(1)} %maximum_bitcast_fusion), channel_id=1, source_target_pairs={{0,4},{4,8},{8,12},{12,16},{16,20},{20,24},{24,28},{28,0},{1,5},{5... | collective-permute-start | bytes 12296 | tf_op jit(solution)/shard_map/ppermute | solution.py:22
  9.2 10.3 %collective-permute-start.5 = (f32[1,2,32]{2,1,0:T(2,128)S(1)}, f32[1,2,32]{2,1,0:T(2,128)S(1)}, u32[]{:S(2)}, u32[]{:S(2)}) collective-permute-start(f32[1,2,32]{2,1,0:T(2,128)S(1)} %pad_maximum_fusion.4), channel_id=1, source_target_pairs={{0,16},{4,20},{8,24},{12,28},{16,0},{20,4},{24,8},{28,12},{1,17},{... | collective-permute-start | bytes 776 | tf_op jit(solution)/shard_map/ppermute | solution.py:33
  12.1 10.5 %all-to-all-start = ((bf16[4,2,2048]{2,1,0:T(2,128)(2,1)}), bf16[4,2,2048]{2,1,0:T(2,128)(2,1)S(1)}, u32[]{:S(2)}, u32[]{:S(2)}) async-start(bf16[4,2,2048]{2,1,0:T(2,128)(2,1)} %reshape.430), calls=%async_computation | async-start | bytes 65536 | tf_op jit(solution)/shard_map/all_to_all | solution.py:185
  28.9 7.2 %collective-permute-start.8 = (f32[2,8,256]{2,1,0:T(8,128)S(1)}, f32[2,8,256]{2,1,0:T(8,128)S(1)}, u32[]{:S(2)}, u32[]{:S(2)}) collective-permute-start(f32[2,8,256]{2,1,0:T(8,128)S(1)} %get-tuple-element.101), channel_id=1, source_target_pairs={{0,3},{1,2},{2,1},{3,0},{4,7},{5,6},{6,5},{7,4},{8,11},{9,10},{10,... | collective-permute-start | bytes 49160 | tf_op jit(solution)/shard_map/ppermute | solution.py:200
  31.3 4.8 %collective-permute-start.7 = (f32[2,8,256]{2,1,0:T(8,128)S(1)}, f32[2,8,256]{2,1,0:T(8,128)S(1)}, u32[]{:S(2)}, u32[]{:S(2)}) collective-permute-start(f32[2,8,256]{2,1,0:T(8,128)S(1)} %get-tuple-element.102), channel_id=1, source_target_pairs={{0,2},{1,3},{2,0},{3,1},{4,6},{5,7},{6,4},{7,5},{8,10},{9,11},{10,... | collective-permute-start | bytes 49160 | tf_op jit(solution)/shard_map/ppermute | solution.py:200
  36.7 7.9 %collective-permute-start.10 = (f32[1,16,2,32]{3,1,2,0:T(8,128)S(1)}, f32[1,16,2,32]{3,1,2,0:T(8,128)S(1)}, u32[]{:S(2)}, u32[]{:S(2)}) collective-permute-start(f32[1,16,2,32]{3,1,2,0:T(8,128)S(1)} %maximum_bitcast_fusion.1), channel_id=1, source_target_pairs={{4,0},{8,4},{12,8},{16,12},{20,16},{24,20},{28,24},{0,28},{5,1},{9... | collective-permute-start | bytes 12296 | tf_op jit(solution)/shard_map/ppermute | solution.py:24
  36.8 7.8 %collective-permute-start.9 = (f32[1,16,2,32]{3,1,2,0:T(8,128)S(1)}, f32[1,16,2,32]{3,1,2,0:T(8,128)S(1)}, u32[]{:S(2)}, u32[]{:S(2)}) collective-permute-start(f32[1,16,2,32]{3,1,2,0:T(8,128)S(1)} %maximum_bitcast_fusion.1), channel_id=1, source_target_pairs={{0,4},{4,8},{8,12},{12,16},{16,20},{20,24},{24,28},{28,0},{1,5},{5... | collective-permute-start | bytes 12296 | tf_op jit(solution)/shard_map/ppermute | solution.py:22
  37.4 7.1 %collective-permute-start.11 = (f32[16,2,32]{2,1,0:T(2,128)S(1)}, f32[16,2,32]{2,1,0:T(2,128)S(1)}, u32[]{:S(2)}, u32[]{:S(2)}) collective-permute-start(f32[16,2,32]{2,1,0:T(2,128)S(1)} %pad_maximum_fusion.1), channel_id=1, source_target_pairs={{0,16},{4,20},{8,24},{12,28},{16,0},{20,4},{24,8},{28,12},{1,17},{... | collective-permute-start | bytes 12296 | tf_op jit(solution)/shard_map/ppermute | solution.py:33
  41.2 8.9 %all-to-all-start.1 = ((bf16[4,2,2048]{2,1,0:T(2,128)(2,1)}), bf16[4,2,2048]{2,1,0:T(2,128)(2,1)S(1)}, u32[]{:S(2)}, u32[]{:S(2)}) async-start(bf16[4,2,2048]{2,1,0:T(2,128)(2,1)} %reshape.432), calls=%async_computation.1 | async-start | bytes 65536 | tf_op jit(solution)/shard_map/all_to_all | solution.py:185
  55.8 6.9 %collective-permute-start.14 = (f32[2,8,256]{2,1,0:T(8,128)}, f32[2,8,256]{2,1,0:T(8,128)S(1)}, u32[]{:S(2)}, u32[]{:S(2)}) collective-permute-start(f32[2,8,256]{2,1,0:T(8,128)} %get-tuple-element.97), channel_id=1, source_target_pairs={{0,3},{1,2},{2,1},{3,0},{4,7},{5,6},{6,5},{7,4},{8,11},{9,10},{10,... | collective-permute-start | bytes 49160 | tf_op jit(solution)/shard_map/ppermute | solution.py:200
  57.3 4.8 %collective-permute-start.13 = (f32[2,8,256]{2,1,0:T(8,128)}, f32[2,8,256]{2,1,0:T(8,128)S(1)}, u32[]{:S(2)}, u32[]{:S(2)}) collective-permute-start(f32[2,8,256]{2,1,0:T(8,128)} %get-tuple-element.98), channel_id=1, source_target_pairs={{0,2},{1,3},{2,0},{3,1},{4,6},{5,7},{6,4},{7,5},{8,10},{9,11},{10,... | collective-permute-start | bytes 49160 | tf_op jit(solution)/shard_map/ppermute | solution.py:200
  65.4 7.2 %collective-permute-start.16 = (f32[1,16,2,32]{3,1,2,0:T(8,128)S(1)}, f32[1,16,2,32]{3,1,2,0:T(8,128)S(1)}, u32[]{:S(2)}, u32[]{:S(2)}) collective-permute-start(f32[1,16,2,32]{3,1,2,0:T(8,128)S(1)} %maximum_bitcast_fusion.2), channel_id=1, source_target_pairs={{4,0},{8,4},{12,8},{16,12},{20,16},{24,20},{28,24},{0,28},{5,1},{9... | collective-permute-start | bytes 12296 | tf_op jit(solution)/shard_map/ppermute | solution.py:24
  65.5 6.7 %collective-permute-start.15 = (f32[1,16,2,32]{3,1,2,0:T(8,128)S(1)}, f32[1,16,2,32]{3,1,2,0:T(8,128)S(1)}, u32[]{:S(2)}, u32[]{:S(2)}) collective-permute-start(f32[1,16,2,32]{3,1,2,0:T(8,128)S(1)} %maximum_bitcast_fusion.2), channel_id=1, source_target_pairs={{0,4},{4,8},{8,12},{12,16},{16,20},{20,24},{24,28},{28,0},{1,5},{5... | collective-permute-start | bytes 12296 | tf_op jit(solution)/shard_map/ppermute | solution.py:22
  66.1 6.0 %collective-permute-start.17 = (f32[16,2,32]{2,1,0:T(2,128)S(1)}, f32[16,2,32]{2,1,0:T(2,128)S(1)}, u32[]{:S(2)}, u32[]{:S(2)}) collective-permute-start(f32[16,2,32]{2,1,0:T(2,128)S(1)} %pad_maximum_fusion.2), channel_id=1, source_target_pairs={{0,16},{4,20},{8,24},{12,28},{16,0},{20,4},{24,8},{28,12},{1,17},{... | collective-permute-start | bytes 12296 | tf_op jit(solution)/shard_map/ppermute | solution.py:33
  68.2 9.5 %all-to-all-start.2 = ((bf16[4,2,2048]{2,1,0:T(2,128)(2,1)}), bf16[4,2,2048]{2,1,0:T(2,128)(2,1)S(1)}, u32[]{:S(2)}, u32[]{:S(2)}) async-start(bf16[4,2,2048]{2,1,0:T(2,128)(2,1)} %reshape.434), calls=%async_computation.2 | async-start | bytes 65536 | tf_op jit(solution)/shard_map/all_to_all | solution.py:185
  83.7 6.1 %collective-permute-start.20 = (f32[2,8,256]{2,1,0:T(8,128)S(1)}, f32[2,8,256]{2,1,0:T(8,128)S(1)}, u32[]{:S(2)}, u32[]{:S(2)}) collective-permute-start(f32[2,8,256]{2,1,0:T(8,128)S(1)} %get-tuple-element.93), channel_id=1, source_target_pairs={{0,3},{1,2},{2,1},{3,0},{4,7},{5,6},{6,5},{7,4},{8,11},{9,10},{10,... | collective-permute-start | bytes 49160 | tf_op jit(solution)/shard_map/ppermute | solution.py:200
  92.0 9.4 %all-to-all-start.3 = ((bf16[4,2,2048]{2,1,0:T(2,128)(2,1)}), bf16[4,2,2048]{2,1,0:T(2,128)(2,1)S(1)}, u32[]{:S(2)}, u32[]{:S(2)}) async-start(bf16[4,2,2048]{2,1,0:T(2,128)(2,1)} %reshape.436), calls=%async_computation.3 | async-start | bytes 65536 | tf_op jit(solution)/shard_map/all_to_all | solution.py:185
  118.6 9.3 %collective-permute-start.28 = (f32[208,640]{1,0:T(8,128)S(1)}, f32[208,640]{1,0:T(8,128)S(1)}, u32[]{:S(2)}, u32[]{:S(2)}) collective-permute-start(f32[208,640]{1,0:T(8,128)S(1)} %dynamic-slice_bitcast_fusion.1), channel_id=1, source_target_pairs={{0,8},{4,20},{8,0},{12,28},{16,24},{20,4},{24,16},{28,12},{1,9},{5... | collective-permute-start | bytes 1597448 | tf_op jit(solution)/shard_map/ppermute | solution.py:116
  128.1 6.5 %collective-permute-start.29 = (f32[104,640]{1,0:T(8,128)S(1)}, f32[104,640]{1,0:T(8,128)S(1)}, u32[]{:S(2)}, u32[]{:S(2)}) collective-permute-start(f32[104,640]{1,0:T(8,128)S(1)} %dynamic-slice_bitcast_fusion.2), channel_id=1, source_target_pairs={{0,16},{4,12},{8,24},{12,4},{16,0},{20,28},{24,8},{28,20},{1,17},{... | collective-permute-start | bytes 798728 | tf_op jit(solution)/shard_map/ppermute | solution.py:116
  134.6 6.8 %collective-permute-start.30 = (f32[104,640]{1,0:T(8,128)S(1)}, f32[104,640]{1,0:T(8,128)S(1)}, u32[]{:S(2)}, u32[]{:S(2)}) collective-permute-start(f32[104,640]{1,0:T(8,128)S(1)} %bitcast_add_fusion.2), channel_id=1, source_target_pairs={{0,1},{1,0},{2,3},{3,2},{4,5},{5,4},{6,7},{7,6},{8,9},{9,8},{10,11... | collective-permute-start | bytes 798728 | tf_op jit(solution)/shard_map/ppermute | solution.py:116
  141.4 12.5 %collective-permute-start.31 = (f32[104,640]{1,0:T(8,128)S(1)}, f32[104,640]{1,0:T(8,128)S(1)}, u32[]{:S(2)}, u32[]{:S(2)}) collective-permute-start(f32[104,640]{1,0:T(8,128)S(1)} %add.439), channel_id=1, source_target_pairs={{0,2},{1,3},{2,0},{3,1},{4,6},{5,7},{6,4},{7,5},{8,10},{9,11},{10,... | collective-permute-start | bytes 798728 | tf_op jit(solution)/shard_map/ppermute | solution.py:116
  153.9 6.7 %collective-permute-start.32 = (f32[104,640]{1,0:T(8,128)S(1)}, f32[104,640]{1,0:T(8,128)S(1)}, u32[]{:S(2)}, u32[]{:S(2)}) collective-permute-start(f32[104,640]{1,0:T(8,128)S(1)} %add.440), channel_id=1, source_target_pairs={{0,16},{4,12},{8,24},{12,4},{16,0},{20,28},{24,8},{28,20},{1,17},{... | collective-permute-start | bytes 798728 | tf_op jit(solution)/shard_map/ppermute | solution.py:116
  155.5 14.7 %collective-permute-start.21 = (f32[1,16,2,32]{3,1,2,0:T(8,128)S(1)}, f32[1,16,2,32]{3,1,2,0:T(8,128)S(1)}, u32[]{:S(2)}, u32[]{:S(2)}) collective-permute-start(f32[1,16,2,32]{3,1,2,0:T(8,128)S(1)} %maximum_bitcast_fusion.3), channel_id=1, source_target_pairs={{0,4},{4,8},{8,12},{12,16},{16,20},{20,24},{24,28},{28,0},{1,5},{5... | collective-permute-start | bytes 12296 | tf_op jit(solution)/shard_map/ppermute | solution.py:22
  155.5 7.2 %collective-permute-start.22 = (f32[1,16,2,32]{3,1,2,0:T(8,128)S(1)}, f32[1,16,2,32]{3,1,2,0:T(8,128)S(1)}, u32[]{:S(2)}, u32[]{:S(2)}) collective-permute-start(f32[1,16,2,32]{3,1,2,0:T(8,128)S(1)} %maximum_bitcast_fusion.3), channel_id=1, source_target_pairs={{4,0},{8,4},{12,8},{16,12},{20,16},{24,20},{28,24},{0,28},{5,1},{9... | collective-permute-start | bytes 12296 | tf_op jit(solution)/shard_map/ppermute | solution.py:24
  160.6 9.3 %collective-permute-start.33 = (f32[208,640]{1,0:T(8,128)S(1)}, f32[208,640]{1,0:T(8,128)S(1)}, u32[]{:S(2)}, u32[]{:S(2)}) collective-permute-start(f32[208,640]{1,0:T(8,128)S(1)} %bitcast.178), channel_id=1, source_target_pairs={{0,8},{4,20},{8,0},{12,28},{16,24},{20,4},{24,16},{28,12},{1,9},{5... | collective-permute-start | bytes 1597448 | tf_op jit(solution)/shard_map/ppermute | solution.py:116
  170.0 10.7 %collective-permute-start.34 = (f32[416,640]{1,0:T(8,128)S(1)}, f32[416,640]{1,0:T(8,128)S(1)}, u32[]{:S(2)}, u32[]{:S(2)}) collective-permute-start(f32[416,640]{1,0:T(8,128)S(1)} %bitcast.174), channel_id=1, source_target_pairs={{0,4},{4,0},{8,12},{12,8},{16,20},{20,16},{24,28},{28,24},{1,5},{5... | collective-permute-start | bytes 3194888 | tf_op jit(solution)/shard_map/ppermute | solution.py:116
  172.4 5.3 %collective-permute-start.24 = (f32[2,8,256]{2,1,0:T(8,128)S(1)}, f32[2,8,256]{2,1,0:T(8,128)S(1)}, u32[]{:S(2)}, u32[]{:S(2)}) collective-permute-start(f32[2,8,256]{2,1,0:T(8,128)S(1)} %get-tuple-element.91), channel_id=1, source_target_pairs={{0,1},{1,0},{2,3},{3,2},{4,5},{5,4},{6,7},{7,6},{8,9},{9,8},{10,11... | collective-permute-start | bytes 49160 | tf_op jit(solution)/shard_map/ppermute | solution.py:200
  174.2 5.8 %collective-permute-start.26 = (f32[2,8,256]{2,1,0:T(8,128)S(1)}, f32[2,8,256]{2,1,0:T(8,128)S(1)}, u32[]{:S(2)}, u32[]{:S(2)}) collective-permute-start(f32[2,8,256]{2,1,0:T(8,128)S(1)} %get-tuple-element.89), channel_id=1, source_target_pairs={{0,3},{1,2},{2,1},{3,0},{4,7},{5,6},{6,5},{7,4},{8,11},{9,10},{10,... | collective-permute-start | bytes 49160 | tf_op jit(solution)/shard_map/ppermute | solution.py:200
  175.3 4.8 %collective-permute-start.25 = (f32[2,8,256]{2,1,0:T(8,128)S(1)}, f32[2,8,256]{2,1,0:T(8,128)S(1)}, u32[]{:S(2)}, u32[]{:S(2)}) collective-permute-start(f32[2,8,256]{2,1,0:T(8,128)S(1)} %get-tuple-element.90), channel_id=1, source_target_pairs={{0,2},{1,3},{2,0},{3,1},{4,6},{5,7},{6,4},{7,5},{8,10},{9,11},{10,... | collective-permute-start | bytes 49160 | tf_op jit(solution)/shard_map/ppermute | solution.py:200
  (38 other events, 219.4 us)
